TPU v7x, 256 devices: a whole 4x4x8 slice. The times are simulated.
256 devices in a mesh: dp: 32 (over y, z), cent: 8 (over x, core).
Axes of the slice: x: 4, y: 4, z: 8, core: 2. Of those that a mesh axis runs over, the one named last changes fastest.
Arguments:
- embeddings: bfloat16 [16384, 768], P('dp'), may hold values from -400 to 400, as said below
- centroids: bfloat16 [16384, 768], P('cent'), may hold values from -400 to 400, as said below
Outputs:
- new_centroids: float32 [16384, 768], P(('cent', 'dp'))
Inputs may be any that keep to these rules, and one draw needn't show every extreme that they name: `embeddings`: finite real values. `centroids`: finite real values.
All inputs are finite; a program needn't handle non-finite values.
Results may differ from a plain program's by a relative error of at most 0.0038.
Values sent between devices are 32-bit elements; how exact they have to be, the bound alone decides.
A program may use at most 64 MiB of HBM per device.

v0:
```python
import jax
import jax.numpy as jnp
from jax import lax
from jax.sharding import PartitionSpec as P

FEATURE_DIM = 768
ROUNDS = 2
entropy_regularizer = 0.05


def normalize(values):
    wide = values.astype(jnp.float32)
    meansq = jnp.mean(wide * wide, axis=-1, keepdims=True)
    return (wide * lax.rsqrt(meansq + 1e-06)).astype(jnp.bfloat16)


def row_update(boltzmann_affinity, column_factor):
    partial_rows = jnp.dot(boltzmann_affinity, column_factor, precision=lax.Precision.HIGHEST)
    totals = lax.psum(partial_rows, "cent")
    return 1.0 / totals


def shards(embeddings, centroids):
    normed = normalize(embeddings)
    cent_normed = normalize(centroids)
    cosine_matches = lax.dot_general(
        normed, cent_normed, (((1,), (1,)), ((), ())), preferred_element_type=jnp.float32
    )
    boltzmann_affinity = jnp.exp(cosine_matches * (1.0 / (FEATURE_DIM * entropy_regularizer)))
    local_cents = centroids.shape[0]
    row_count = embeddings.shape[0] * lax.axis_size("dp")
    cent_count = local_cents * lax.axis_size("cent")
    balance_ratio = row_count / cent_count
    column_factor = jnp.ones((local_cents,), jnp.float32)
    for sweep in range(ROUNDS):
        row_weight = row_update(boltzmann_affinity, column_factor)
        partial_cols = jnp.dot(row_weight, boltzmann_affinity, precision=lax.Precision.HIGHEST)
        column_factor = balance_ratio / lax.psum(partial_cols, "dp")
    row_weight = row_update(boltzmann_affinity, column_factor)
    transport = (row_weight[:, None] * boltzmann_affinity * column_factor[None, :]).astype(
        jnp.bfloat16
    )
    col_mass = jnp.sum(transport, axis=0, dtype=jnp.float32)
    own_rows = local_cents // lax.axis_size("dp")
    holder_position = lax.axis_index("dp")
    weighted = lax.dot_general(
        transport, normed, (((0,), (0,)), ((), ())), preferred_element_type=jnp.float32
    )
    weighted, col_mass = lax.psum((weighted, col_mass), "dp")
    weighted = lax.dynamic_slice_in_dim(weighted, holder_position * own_rows, own_rows, 0)
    col_mass = lax.dynamic_slice_in_dim(col_mass, holder_position * own_rows, own_rows, 0)
    return weighted / col_mass[:, None]


def solution(mesh):
    in_specs = (P("dp", None), P("cent", None))
    out_specs = P(("cent", "dp"), None)
    return jax.shard_map(shards, mesh=mesh, in_specs=in_specs, out_specs=out_specs, check_vma=False)
```

profile of v0, /device:TPU:1, one launch (start us, length us, event | category | flops | bytes accessed | tf_op | source)
XLA Modules:
  0.0 423.9 jit_solution(16495555627973379805)
XLA Ops:
  6.5 0.0 all-reduce.2.cloned.1.call-start
  6.5 1.4 fusion.4
  7.9 2.6 fusion
  10.5 4.1 multiply_exponential_fusion
  14.6 0.0 copy-start
  14.6 1.9 copy-done
  16.6 3.6 fusion.9
  20.2 15.0 %psum.49 = f32[512]{0:T(512)S(1)} all-reduce(f32[512]{0:T(512)S(1)} %bitcast.25), channel_id=1, replica_groups=mesh['dp'=32,'cent'=8] {'cent'}, use_global_device_ids=true, to_apply=%region_2.0 | all-reduce | flops 512 | bytes 4096 | tf_op jit(solution)/shard_map/psum | solution.py:19
  35.2 4.3 %fusion.12 = f32[1,2048]{1,0:T(1,128)S(1)} fusion(f32[512,1]{0,1:T(1,128)S(1)} %bitcast.22, f32[512,2048]{1,0:T(8,128)} %copy-done), kind=kOutput, calls=%fused_computation.24 | convolution fusion | flops 12582912 | bytes 4204544 | tf_op jit(solution)/shard_map/dot_general | solution.py:37
  39.4 63.4 %psum.50 = f32[2048]{0:T(1024)S(1)} all-reduce(f32[2048]{0:T(1024)S(1)} %bitcast.19), channel_id=1, replica_groups=mesh['dp'=32,'cent'=8] {'dp'}, use_global_device_ids=true, to_apply=%region_3.0 | all-reduce | flops 2048 | bytes 16384 | tf_op jit(solution)/shard_map/psum | solution.py:38
  102.9 5.8 %fusion.13 = f32[1,512]{1,0:T(1,128)S(1)} fusion(f32[512,2048]{1,0:T(8,128)} %copy-done, f32[2048,1]{0,1:T(1,128)S(1)} %bitcast.20), kind=kOutput, calls=%fused_computation.25 | convolution fusion | flops 12582912 | bytes 4204544 | tf_op jit(solution)/shard_map/dot_general | solution.py:18
  108.6 28.6 %psum.51 = f32[512]{0:T(512)S(1)} all-reduce(f32[512]{0:T(512)S(1)} %bitcast.23), channel_id=1, replica_groups=mesh['dp'=32,'cent'=8] {'cent'}, use_global_device_ids=true, to_apply=%region_4.0 | all-reduce | flops 512 | bytes 4096 | tf_op jit(solution)/shard_map/psum | solution.py:19
  137.2 4.3 %fusion.14 = f32[1,2048]{1,0:T(1,128)S(1)} fusion(f32[512,1]{0,1:T(1,128)S(1)} %bitcast.24, f32[512,2048]{1,0:T(8,128)} %copy-done), kind=kOutput, calls=%fused_computation.26 | convolution fusion | flops 12582912 | bytes 4204544 | tf_op jit(solution)/shard_map/dot_general | solution.py:37
  141.6 57.2 %psum.52 = f32[2048]{0:T(1024)S(1)} all-reduce(f32[2048]{0:T(1024)S(1)} %bitcast.21), channel_id=1, replica_groups=mesh['dp'=32,'cent'=8] {'dp'}, use_global_device_ids=true, to_apply=%region_5.0 | all-reduce | flops 2048 | bytes 16384 | tf_op jit(solution)/shard_map/psum | solution.py:38
  198.8 5.8 %fusion.15 = f32[1,512]{1,0:T(1,128)S(1)} fusion(f32[512,2048]{1,0:T(8,128)} %copy-done, f32[2048,1]{0,1:T(1,128)S(1)} %bitcast.18), kind=kOutput, calls=%fused_computation.27 | convolution fusion | flops 12582912 | bytes 4204544 | tf_op jit(solution)/shard_map/dot_general | solution.py:18
  204.6 25.8 %psum.53 = f32[512]{0:T(512)S(1)} all-reduce(f32[512]{0:T(512)S(1)} %bitcast.26), channel_id=1, replica_groups=mesh['dp'=32,'cent'=8] {'cent'}, use_global_device_ids=true, to_apply=%region_6.0 | all-reduce | flops 512 | bytes 4096 | tf_op jit(solution)/shard_map/psum | solution.py:19
  230.4 0.0 copy-done.1
  230.4 6.8 %fusion.6 = f32[2048,768]{1,0:T(8,128)} fusion(bf16[512,768]{1,0:T(8,128)(2,1)S(1)} %copy-done.1, f32[512]{0:T(512)S(1)} %add_rsqrt_fusion.1, f32[512,2048]{1,0:T(8,128)} %copy-done, f32[2048]{0:T(1024)S(1)} %broadcast_divide_fusion.1, f32[512]{0:T(512)S(1)} %broadcast_divide_fusion.2), kind=kOutput, calls=%fused_computation.12 | convolution fusion | flops 1614938112 | bytes 11284480 | tf_op jit(solution)/shard_map/dot_general | solution.py:46
  237.3 0.0 all-reduce.2.cloned.1.call-update
  237.3 2.7 convert_reduce_fusion
  240.0 62.2 %psum.55 = f32[2048]{0:T(1024)S(1)} all-reduce(f32[2048]{0:T(1024)S(1)} %convert_reduce_fusion), channel_id=1, replica_groups=mesh['dp'=32,'cent'=8] {'dp'}, use_global_device_ids=true, to_apply=%region_9.0 | all-reduce | flops 2048 | bytes 16384 | tf_op jit(solution)/shard_map/psum | solution.py:49
  302.2 0.1 dynamic_slice.7
  302.3 113.1 %all-reduce.2.cloned.1.call-done = f32[2048,768]{1,0:T(8,128)} async-done(((f32[2048,768]{1,0:T(8,128)}), f32[2048,768]{1,0:T(8,128)}) %all-reduce.2.cloned.1.call-update) | async-done | bytes 6291472 | tf_op jit(solution)/shard_map/psum | solution.py:49
  415.3 1.7 dynamic-slice_divide_fusion
  (8 shorter events, 0.0 us)
Async XLA Ops:
  6.5 408.8 %all-reduce.2.cloned.1.call-start = ((), (), s32[]{:S(2)}) async-start(), calls=%async_computation | async-start | bytes 12582912 | tf_op jit(solution)/shard_map/psum | solution.py:49
  14.6 2.0 copy-start
  137.2 93.2 %copy-start.1 = (bf16[512,768]{1,0:T(8,128)(2,1)S(1)}, bf16[512,768]{1,0:T(8,128)(2,1)}, u32[]{:S(2)}) copy-start(bf16[512,768]{1,0:T(8,128)(2,1)} %param.2) | copy-start | bytes 2359300
Sparse Core Ops, SparseCore 0:
  237.4 177.8 all-reduce.1
where the time goes:
time: 424 us
  blocking collectives  252 us (59%)
  waiting for transfers between devices  113 us (27%)
  matrix products  34.7 us (8%)
  between operations  13.5 us (3%)
  other arithmetic  8.35 us (2%)
    psum x2, blocking collectives, shards(): column_factor = balance_ratio / lax.psum(partial_cols, 'dp')  121 us
    psum x1, waiting for transfers between devices, shards(): weighted, col_mass = lax.psum((weighted, col_mass), 'dp')  113 us
    psum x3, blocking collectives, row_update(): totals = lax.psum(partial_rows, 'cent')  69.4 us
    psum x1, blocking collectives, shards(): weighted, col_mass = lax.psum((weighted, col_mass), 'dp')  62.2 us
    dot_general x3, matrix products, row_update(): jnp.dot(boltzmann_affinity, column_factor, precision=lax.Precision.HIGHEST)  15.1 us
    dot_general x2, matrix products, shards(): jnp.dot(row_weight, boltzmann_affinity, precision=lax.Precision.HIGHEST)  8.61 us
  transfers between devices with their start and end apart: 1, of which 1 were waited for; matrix products, arithmetic and copies ran while one was open for 1% of the time, Pallas kernels for 0%

commit v1 on v0

--- a/solution.py
+++ b/solution.py
@@ -1,3 +1,4 @@
+import functools
 import jax
 import jax.numpy as jnp
 from jax import lax
@@ -6,6 +7,14 @@
 FEATURE_DIM = 768
 ROUNDS = 2
 entropy_regularizer = 0.05
+
+
+def draft_array(buf, peer_axis):
+    latest = lax.all_gather(buf, peer_axis)
+    return jnp.sum(latest, 0)
+
+
+write_samples_all = functools.partial(draft_array, peer_axis="dp")
 
 
 def normalize(values):
@@ -35,7 +44,7 @@
     for sweep in range(ROUNDS):
         row_weight = row_update(boltzmann_affinity, column_factor)
         partial_cols = jnp.dot(row_weight, boltzmann_affinity, precision=lax.Precision.HIGHEST)
-        column_factor = balance_ratio / lax.psum(partial_cols, "dp")
+        column_factor = balance_ratio / write_samples_all(partial_cols)
     row_weight = row_update(boltzmann_affinity, column_factor)
     transport = (row_weight[:, None] * boltzmann_affinity * column_factor[None, :]).astype(
         jnp.bfloat16

time: 424 us -> 379 us (0.89)
  blocking collectives: 252 us -> 204 us
    psum x2 -> x0, blocking collectives: 121 us -> none  [shards(): column_factor = balance_ratio / lax.psum(partial_cols, 'dp')]
    all_gather x0 -> x2, blocking collectives: none -> 74.4 us  [draft_array(): latest = lax.all_gather(buf, peer_axis)]
where the time goes in v1:
time: 379 us; the launch traced here: 378 us
  blocking collectives  204 us (54%)
  waiting for transfers between devices  115 us (30%)
  matrix products  34.7 us (9%)
  between operations  13.5 us (4%)
  other arithmetic  8.41 us (2%)
    psum x1, waiting for transfers between devices, shards(): weighted, col_mass = lax.psum((weighted, col_mass), 'dp')  115 us
    all_gather x2, blocking collectives, draft_array(): latest = lax.all_gather(buf, peer_axis)  74.4 us
    psum x3, blocking collectives, row_update(): totals = lax.psum(partial_rows, 'cent')  67 us
    psum x1, blocking collectives, shards(): weighted, col_mass = lax.psum((weighted, col_mass), 'dp')  62.5 us
    dot_general x3, matrix products, row_update(): jnp.dot(boltzmann_affinity, column_factor, precision=lax.Precision.HIGHEST)  15.1 us
    dot_general x2, matrix products, shards(): jnp.dot(row_weight, boltzmann_affinity, precision=lax.Precision.HIGHEST)  8.61 us
  transfers between devices with their start and end apart: 1, of which 1 were waited for; matrix products, arithmetic and copies ran while one was open for 1% of the time, Pallas kernels for 0%

profile of v1, /device:TPU:1, one launch (start us, length us, event | category | flops | bytes accessed | tf_op | source)
XLA Modules:
  0.0 378.1 jit_solution(13290354889377410753)
XLA Ops:
  6.5 0.0 all-reduce.2.cloned.1.call-start
  6.5 1.4 fusion.4
  7.9 2.6 fusion
  10.5 4.1 %multiply_exponential_fusion = f32[512,2048]{1,0:T(8,128)S(1)} fusion(bf16[2048,768]{1,0:T(8,128)(2,1)} %param.3, f32[2048]{0:T(1024)S(1)} %add_rsqrt_fusion, bf16[512,768]{1,0:T(8,128)(2,1)} %param.2, f32[512]{0:T(512)S(1)} %add_rsqrt_fusion.1), kind=kOutput, calls=%fused_computation.6 | convolution fusion | flops 1617559552 | bytes 8136704 | tf_op jit(solution)/shard_map/dot_general | solution.py:35
  14.6 0.0 copy-start
  14.6 1.9 copy-done
  16.6 3.6 fusion.9
  20.2 15.0 %psum.35 = f32[512]{0:T(512)S(1)} all-reduce(f32[512]{0:T(512)S(1)} %bitcast.25), channel_id=1, replica_groups=mesh['dp'=32,'cent'=8] {'cent'}, use_global_device_ids=true, to_apply=%region_2.0 | all-reduce | flops 512 | bytes 4096 | tf_op jit(solution)/shard_map/psum | solution.py:28
  35.2 4.3 %fusion.12 = f32[1,2048]{1,0:T(1,128)S(1)} fusion(f32[512,1]{0,1:T(1,128)S(1)} %bitcast.22, f32[512,2048]{1,0:T(8,128)} %copy-done), kind=kOutput, calls=%fused_computation.24 | convolution fusion | flops 12582912 | bytes 4204544 | tf_op jit(solution)/shard_map/dot_general | solution.py:46
  39.4 38.5 %all-gather = f32[65536]{0:T(1024)S(1)} all-gather(f32[2048]{0:T(1024)S(1)} %bitcast.19), channel_id=2, replica_groups=mesh['dp'=32,'cent'=8] {'dp'}, dimensions={0}, use_global_device_ids=true | all-gather | bytes 270336 | tf_op jit(solution)/shard_map/all_gather | solution.py:13
  78.0 5.8 %fusion.13 = f32[1,512]{1,0:T(1,128)S(1)} fusion(f32[512,2048]{1,0:T(8,128)} %copy-done, f32[2048,1]{0,1:T(1,128)S(1)} %bitcast.21), kind=kOutput, calls=%fused_computation.25 | convolution fusion | flops 12582912 | bytes 4204544 | tf_op jit(solution)/shard_map/dot_general | solution.py:27
  83.8 27.2 %psum.36 = f32[512]{0:T(512)S(1)} all-reduce(f32[512]{0:T(512)S(1)} %bitcast.23), channel_id=1, replica_groups=mesh['dp'=32,'cent'=8] {'cent'}, use_global_device_ids=true, to_apply=%region_4.0 | all-reduce | flops 512 | bytes 4096 | tf_op jit(solution)/shard_map/psum | solution.py:28
  111.0 4.3 %fusion.14 = f32[1,2048]{1,0:T(1,128)S(1)} fusion(f32[512,1]{0,1:T(1,128)S(1)} %bitcast.24, f32[512,2048]{1,0:T(8,128)} %copy-done), kind=kOutput, calls=%fused_computation.26 | convolution fusion | flops 12582912 | bytes 4204544 | tf_op jit(solution)/shard_map/dot_general | solution.py:46
  115.4 35.9 %all-gather.1 = f32[65536]{0:T(1024)S(1)} all-gather(f32[2048]{0:T(1024)S(1)} %bitcast.20), channel_id=3, replica_groups=mesh['dp'=32,'cent'=8] {'dp'}, dimensions={0}, use_global_device_ids=true | all-gather | bytes 270336 | tf_op jit(solution)/shard_map/all_gather | solution.py:13
  151.4 5.8 %fusion.15 = f32[1,512]{1,0:T(1,128)S(1)} fusion(f32[512,2048]{1,0:T(8,128)} %copy-done, f32[2048,1]{0,1:T(1,128)S(1)} %bitcast.18), kind=kOutput, calls=%fused_computation.27 | convolution fusion | flops 12582912 | bytes 4204544 | tf_op jit(solution)/shard_map/dot_general | solution.py:27
  157.2 24.7 %psum.37 = f32[512]{0:T(512)S(1)} all-reduce(f32[512]{0:T(512)S(1)} %bitcast.26), channel_id=1, replica_groups=mesh['dp'=32,'cent'=8] {'cent'}, use_global_device_ids=true, to_apply=%region_6.0 | all-reduce | flops 512 | bytes 4096 | tf_op jit(solution)/shard_map/psum | solution.py:28
  181.9 0.0 copy-done.1
  181.9 6.8 %fusion.6 = f32[2048,768]{1,0:T(8,128)} fusion(bf16[512,768]{1,0:T(8,128)(2,1)S(1)} %copy-done.1, f32[512]{0:T(512)S(1)} %add_rsqrt_fusion.1, f32[512,2048]{1,0:T(8,128)} %copy-done, f32[2048]{0:T(1024)S(1)} %broadcast_divide_fusion.1, f32[512]{0:T(512)S(1)} %broadcast_divide_fusion.2), kind=kOutput, calls=%fused_computation.12 | convolution fusion | flops 1614938112 | bytes 11284480 | tf_op jit(solution)/shard_map/dot_general | solution.py:55
  188.8 0.0 all-reduce.2.cloned.1.call-update
  188.8 2.7 convert_reduce_fusion
  191.5 62.5 %psum.39 = f32[2048]{0:T(1024)S(1)} all-reduce(f32[2048]{0:T(1024)S(1)} %convert_reduce_fusion), channel_id=1, replica_groups=mesh['dp'=32,'cent'=8] {'dp'}, use_global_device_ids=true, to_apply=%region_9.0 | all-reduce | flops 2048 | bytes 16384 | tf_op jit(solution)/shard_map/psum | solution.py:58
  254.0 0.1 dynamic_slice.7
  254.1 115.4 %all-reduce.2.cloned.1.call-done = f32[2048,768]{1,0:T(8,128)} async-done(((f32[2048,768]{1,0:T(8,128)}), f32[2048,768]{1,0:T(8,128)}) %all-reduce.2.cloned.1.call-update) | async-done | bytes 6291472 | tf_op jit(solution)/shard_map/psum | solution.py:58
  369.5 1.7 dynamic-slice_divide_fusion
  (12 shorter events, 0.2 us)
Async XLA Ops:
  6.5 363.0 %all-reduce.2.cloned.1.call-start = ((), (), s32[]{:S(2)}) async-start(), calls=%async_computation | async-start | bytes 12582912 | tf_op jit(solution)/shard_map/psum | solution.py:58
  14.6 2.0 copy-start
  111.0 70.9 %copy-start.1 = (bf16[512,768]{1,0:T(8,128)(2,1)S(1)}, bf16[512,768]{1,0:T(8,128)(2,1)}, u32[]{:S(2)}) copy-start(bf16[512,768]{1,0:T(8,128)(2,1)} %param.2) | copy-start | bytes 2359300
Sparse Core Ops, SparseCore 0:
  188.9 180.5 all-reduce.1
